TPU v7x, 32 devices: a whole 2x2x4 slice. The times are simulated.
32 devices in a mesh: rows: 8 (over z, x), seq: 4 (over y, core).
Axes of the slice: x: 2, y: 2, z: 4, core: 2. Of those that a mesh axis runs over, the one named last changes fastest.
Arguments:
- inputs: bfloat16 [8, 2048, 1024], P('rows', 'seq'), may hold values from -6 to 6
- skip_feats: bfloat16 [8, 2048, 1024], P('rows', 'seq'), may hold values from -6 to 6
- seg_ids: int32 [8, 2048], P('rows'), may hold values from 0 to 5, never falling along the last dimension, each value on 1 to 682 neighbouring positions
- frame_valid: int32 [8, 2048], P('rows'), may hold values 0 or 1
- w_skip: bfloat16 [2048, 1024], replicated, may hold values from -0.125 to 0.125
- gain_one: bfloat16 [1024], replicated, may hold values from 0.5 to 1.5
- w_qkv: bfloat16 [1024, 3072], replicated, may hold values from -0.1875 to 0.1875
- w_out: bfloat16 [1024, 1024], replicated, may hold values from -0.5 to 0.5
- gain_two: bfloat16 [1024], replicated, may hold values from 0.5 to 1.5
- w_up: bfloat16 [1024, 4096], replicated, may hold values from -0.1875 to 0.1875
- b_up: bfloat16 [4096], replicated, may hold values from -3 to 3
- w_down: bfloat16 [4096, 1024], replicated, may hold values from -0.09375 to 0.09375
- b_down: bfloat16 [1024], replicated, may hold values from -2 to 2
- cotangent: bfloat16 [8, 2048, 1024], P('rows', 'seq'), may hold values from -6 to 6
Outputs:
- output: bfloat16 [8, 2048, 1024], P('rows', 'seq')
- input_grad: bfloat16 [8, 2048, 1024], P('rows', 'seq')
- skip_grad: bfloat16 [8, 2048, 1024], P('rows', 'seq')
- w_skip_grad: float32 [2048, 1024], P(('rows', 'seq'))
- gain_one_grad: float32 [1024], P(('rows', 'seq'))
- w_qkv_grad: float32 [1024, 3072], P(('rows', 'seq'))
- w_out_grad: float32 [1024, 1024], P(('rows', 'seq'))
- gain_two_grad: float32 [1024], P(('rows', 'seq'))
- w_up_grad: float32 [1024, 4096], P(('rows', 'seq'))
- b_up_grad: float32 [4096], P(('rows', 'seq'))
- w_down_grad: float32 [4096, 1024], P(('rows', 'seq'))
- b_down_grad: float32 [1024], P(('rows', 'seq'))
Inputs may be any that keep to these rules, and one draw needn't show every extreme that they name: `seg_ids`: in each row the segment numbers never fall along the frames; every segment has 1 to 682 frames and one has exactly 682.
All inputs are finite; a program needn't handle non-finite values. No bound on the sum of `frame_valid` on one device may be relied on, other than what follows from the above.
Results may differ from a plain program's by a relative error of at most 0.015.
Values may be sent and summed in bfloat16 or wider, within the bound.
A program may use at most 192 MiB of HBM per device.

v0:
```python
import math
import jax
import jax.numpy as jnp
from jax import lax
from jax.sharding import PartitionSpec as P

D = 1024
H = 16
HD = 64
epsilon = 1e-05


def norm_forward(value, gain_vec):
    center = value - jnp.mean(value, axis=-1, keepdims=True)
    spread = jnp.mean(center * center, axis=-1, keepdims=True)
    inverse = lax.rsqrt(spread + epsilon)
    unit = center * inverse
    return (unit, inverse, unit * gain_vec)


def norm_backward(upstream, unit, inverse, gain_vec):
    scaled = upstream * gain_vec
    gain_grad = jnp.sum(upstream * unit, axis=(0, 1))
    inner = (
        scaled
        - jnp.mean(scaled, axis=-1, keepdims=True)
        - unit * jnp.mean(scaled * unit, axis=-1, keepdims=True)
    )
    return (inverse * inner, gain_grad)


def gelu_exact(value):
    return jax.nn.gelu(value, approximate=False)


def block_scores(q_blk, pos_blk, seg_blk, all_keys, seg_row, valid_row, slopes, score_scale):
    key_pos = jnp.arange(all_keys.shape[0])
    scores = (
        jnp.einsum("qhd,khd->hqk", q_blk, all_keys, preferred_element_type=jnp.float32)
        * score_scale
    )
    distance = jnp.abs(pos_blk[:, None] - key_pos[None, :]).astype(jnp.float32)
    scores = scores - slopes[:, None, None] * distance[None]
    allowed = (seg_blk[:, None] == seg_row[None, :]) & (
        (valid_row[None, :] == 1) | (pos_blk[:, None] == key_pos[None, :])
    )
    return jnp.where(allowed[None], scores, -jnp.inf)


def split_row(packed_row, heads_local):
    length = packed_row.shape[0]
    qkv_rows = packed_row.reshape(length, 3, heads_local, HD)
    return (qkv_rows[:, 0], qkv_rows[:, 1], qkv_rows[:, 2])


def attend_row(packed_row, seg_row, valid_row, slopes, heads_local, block_rows, score_scale):
    length = packed_row.shape[0]
    queries, all_keys, all_values = split_row(packed_row, heads_local)
    count = length // block_rows
    positions = jnp.arange(length)

    def one_block(block_in):
        q_blk, pos_blk, seg_blk = block_in
        scores = block_scores(
            q_blk, pos_blk, seg_blk, all_keys, seg_row, valid_row, slopes, score_scale
        )
        peak = jnp.max(scores, axis=-1, keepdims=True)
        log_total = peak + jnp.log(jnp.sum(jnp.exp(scores - peak), axis=-1, keepdims=True))
        attn_probs = jnp.exp(scores - log_total).astype(jnp.bfloat16)
        attended = jnp.einsum(
            "hqk,khd->qhd", attn_probs, all_values, preferred_element_type=jnp.float32
        )
        return (attended.astype(jnp.bfloat16), log_total[..., 0])

    attended, log_total = lax.map(
        one_block,
        (
            queries.reshape(count, block_rows, heads_local, HD),
            positions.reshape(count, block_rows),
            seg_row.reshape(count, block_rows),
        ),
    )
    return (attended.reshape(length, 1, heads_local * HD), log_total)


def attend_row_back(
    packed_row,
    log_total,
    grad_row,
    seg_row,
    valid_row,
    slopes,
    heads_local,
    block_rows,
    score_scale,
):
    length = packed_row.shape[0]
    queries, all_keys, all_values = split_row(packed_row, heads_local)
    count = length // block_rows
    positions = jnp.arange(length)
    grad_out = grad_row.reshape(count, block_rows, heads_local, HD)

    def one_block(carry, block_in):
        key_grad, value_grad = carry
        q_blk, pos_blk, seg_blk, total_blk, grad_blk = block_in
        scores = block_scores(
            q_blk, pos_blk, seg_blk, all_keys, seg_row, valid_row, slopes, score_scale
        )
        soft = jnp.exp(scores - total_blk[..., None])
        value_grad = value_grad + jnp.einsum(
            "hqk,qhd->khd", soft.astype(jnp.bfloat16), grad_blk, preferred_element_type=jnp.float32
        )
        prob_grad = jnp.einsum(
            "qhd,khd->hqk", grad_blk, all_values, preferred_element_type=jnp.float32
        )
        score_grad = (
            soft * (prob_grad - jnp.sum(soft * prob_grad, axis=-1, keepdims=True))
        ).astype(jnp.bfloat16)
        query_grad = (
            jnp.einsum("hqk,khd->qhd", score_grad, all_keys, preferred_element_type=jnp.float32)
            * score_scale
        )
        key_grad = (
            key_grad
            + jnp.einsum("hqk,qhd->khd", score_grad, q_blk, preferred_element_type=jnp.float32)
            * score_scale
        )
        return ((key_grad, value_grad), query_grad)

    zero_rows = jnp.zeros((length, heads_local, HD), jnp.float32)
    (key_grad, value_grad), query_grad = lax.scan(
        one_block,
        (zero_rows, zero_rows),
        (
            queries.reshape(count, block_rows, heads_local, HD),
            positions.reshape(count, block_rows),
            seg_row.reshape(count, block_rows),
            log_total,
            grad_out,
        ),
    )
    stacked = jnp.stack([query_grad.reshape(length, heads_local, HD), key_grad, value_grad], axis=1)
    return stacked.astype(jnp.bfloat16).reshape(length, 3, 1, heads_local * HD)


def body(
    inputs,
    skip_feats,
    seg_ids,
    frame_valid,
    w_skip,
    gain_one,
    w_qkv,
    w_out,
    gain_two,
    w_up,
    b_up,
    w_down,
    b_down,
    cotangent,
):
    parts = lax.axis_size("seq")
    heads_local = H // parts
    width_local = heads_local * HD
    rows_here = inputs.shape[0]
    frames = inputs.shape[1]
    length = frames * parts
    block_rows = min(512, length)
    score_scale = 1.0 / math.sqrt(HD)
    first_head = lax.axis_index("seq") * heads_local
    slopes = jnp.exp2(-8.0 * (first_head + jnp.arange(heads_local) + 1).astype(jnp.float32) / H)
    gain_first = gain_one.astype(jnp.float32)
    gain_second = gain_two.astype(jnp.float32)
    bias_up = b_up.astype(jnp.float32)
    joined = jnp.concatenate([inputs, skip_feats], axis=-1)
    stem_out = jnp.einsum("rfc,cd->rfd", joined, w_skip, preferred_element_type=jnp.float32)
    unit_one, inverse_one, normed = norm_forward(stem_out, gain_first)
    normed = normed.astype(jnp.bfloat16)
    packed = jnp.einsum("rfd,de->rfe", normed, w_qkv, preferred_element_type=jnp.float32).astype(
        jnp.bfloat16
    )
    packed = packed.reshape(rows_here, frames, 3, parts, width_local)
    by_heads = lax.all_to_all(packed, "seq", split_axis=3, concat_axis=1, tiled=True)

    def forward_row(row_data):
        return attend_row(
            row_data[0], row_data[1], row_data[2], slopes, heads_local, block_rows, score_scale
        )

    attended, log_total = lax.map(forward_row, (by_heads, seg_ids, frame_valid))
    by_frames = lax.all_to_all(attended, "seq", split_axis=1, concat_axis=2, tiled=True)
    mixed_out = by_frames.reshape(rows_here, frames, D)
    middle = stem_out + jnp.einsum(
        "rfd,de->rfe", mixed_out, w_out, preferred_element_type=jnp.float32
    )
    unit_two, inverse_two, second = norm_forward(middle, gain_second)
    second = second.astype(jnp.bfloat16)
    hidden = jnp.einsum("rfd,dk->rfk", second, w_up, preferred_element_type=jnp.float32) + bias_up
    active_full, gelu_back = jax.vjp(gelu_exact, hidden)
    active = active_full.astype(jnp.bfloat16)
    result = (
        middle
        + jnp.einsum("rfk,kd->rfd", active, w_down, preferred_element_type=jnp.float32)
        + b_down.astype(jnp.float32)
    )
    output = result.astype(jnp.bfloat16)
    cot_full = cotangent.astype(jnp.float32)
    down_grad = jnp.einsum("rfk,rfd->kd", active, cotangent, preferred_element_type=jnp.float32)
    bias_down_grad = jnp.sum(cot_full, axis=(0, 1))
    active_grad = jnp.einsum("rfd,kd->rfk", cotangent, w_down, preferred_element_type=jnp.float32)
    hidden_grad = gelu_back(active_grad)[0].astype(jnp.bfloat16)
    up_grad = jnp.einsum("rfd,rfk->dk", second, hidden_grad, preferred_element_type=jnp.float32)
    bias_up_grad = jnp.sum(hidden_grad.astype(jnp.float32), axis=(0, 1))
    second_grad = jnp.einsum("rfk,dk->rfd", hidden_grad, w_up, preferred_element_type=jnp.float32)
    middle_part, gain_two_grad = norm_backward(second_grad, unit_two, inverse_two, gain_second)
    middle_grad = cot_full + middle_part
    middle_low = middle_grad.astype(jnp.bfloat16)
    out_grad = jnp.einsum("rfd,rfe->de", mixed_out, middle_low, preferred_element_type=jnp.float32)
    mixed_grad = jnp.einsum(
        "rfe,de->rfd", middle_low, w_out, preferred_element_type=jnp.float32
    ).astype(jnp.bfloat16)
    grad_heads = lax.all_to_all(
        mixed_grad.reshape(rows_here, frames, parts, width_local),
        "seq",
        split_axis=2,
        concat_axis=1,
        tiled=True,
    )

    def backward_row(row_data):
        return attend_row_back(
            row_data[0],
            row_data[1],
            row_data[2],
            row_data[3],
            row_data[4],
            slopes,
            heads_local,
            block_rows,
            score_scale,
        )

    packed_grad = lax.map(backward_row, (by_heads, log_total, grad_heads, seg_ids, frame_valid))
    packed_back = lax.all_to_all(packed_grad, "seq", split_axis=1, concat_axis=3, tiled=True)
    packed_back = packed_back.reshape(rows_here, frames, 3 * D)
    qkv_grad = jnp.einsum("rfd,rfe->de", normed, packed_back, preferred_element_type=jnp.float32)
    normed_grad = jnp.einsum("rfe,de->rfd", packed_back, w_qkv, preferred_element_type=jnp.float32)
    stem_part, gain_one_grad = norm_backward(normed_grad, unit_one, inverse_one, gain_first)
    stem_low = (middle_grad + stem_part).astype(jnp.bfloat16)
    skip_w_grad = jnp.einsum("rfc,rfd->cd", joined, stem_low, preferred_element_type=jnp.float32)
    joined_grad = jnp.einsum("rfd,cd->rfc", stem_low, w_skip, preferred_element_type=jnp.float32)
    input_grad = joined_grad[..., :D].astype(jnp.bfloat16)
    skip_grad = joined_grad[..., D:].astype(jnp.bfloat16)
    (
        skip_share,
        gain_one_share,
        qkv_share,
        out_share,
        gain_two_share,
        up_share,
        bias_up_share,
        down_share,
        bias_down_share,
    ) = (
        lax.psum_scatter(skip_w_grad, ("rows", "seq"), scatter_dimension=0, tiled=True),
        lax.psum_scatter(gain_one_grad, ("rows", "seq"), scatter_dimension=0, tiled=True),
        lax.psum_scatter(qkv_grad, ("rows", "seq"), scatter_dimension=0, tiled=True),
        lax.psum_scatter(out_grad, ("rows", "seq"), scatter_dimension=0, tiled=True),
        lax.psum_scatter(gain_two_grad, ("rows", "seq"), scatter_dimension=0, tiled=True),
        lax.psum_scatter(up_grad, ("rows", "seq"), scatter_dimension=0, tiled=True),
        lax.psum_scatter(bias_up_grad, ("rows", "seq"), scatter_dimension=0, tiled=True),
        lax.psum_scatter(down_grad, ("rows", "seq"), scatter_dimension=0, tiled=True),
        lax.psum_scatter(bias_down_grad, ("rows", "seq"), scatter_dimension=0, tiled=True),
    )
    return (
        output,
        input_grad,
        skip_grad,
        skip_share,
        gain_one_share,
        qkv_share,
        out_share,
        gain_two_share,
        up_share,
        bias_up_share,
        down_share,
        bias_down_share,
    )


def solution(mesh):
    return jax.shard_map(
        body,
        mesh=mesh,
        in_specs=(
            P("rows", "seq", None),
            P("rows", "seq", None),
            P("rows", None),
            P("rows", None),
            P(),
            P(),
            P(),
            P(),
            P(),
            P(),
            P(),
            P(),
            P(),
            P("rows", "seq", None),
        ),
        out_specs=(
            P("rows", "seq", None),
            P("rows", "seq", None),
            P("rows", "seq", None),
            P(("rows", "seq"), None),
            P(("rows", "seq")),
            P(("rows", "seq"), None),
            P(("rows", "seq"), None),
            P(("rows", "seq")),
            P(("rows", "seq"), None),
            P(("rows", "seq")),
            P(("rows", "seq"), None),
            P(("rows", "seq")),
        ),
        check_vma=False,
    )
```

profile of v0, /device:TPU:3, one launch (start us, length us, event | category | flops | bytes accessed | tf_op | source)
XLA Modules:
  0.0 1326.1 jit_solution(4575809649064550022)
XLA Ops:
  7.2 5.4 fusion.74
  14.6 5.2 convolution_convert_fusion
  19.8 6.7 reshape.605
  30.5 5.4 all-to-all-start
  37.1 35.0 %all-to-all-done = bf16[1,512,3,4,256]{4,1,2,0,3:T(8,128)(2,1)} async-done(((bf16[1,512,3,4,256]{4,1,2,0,3:T(8,128)(2,1)}), bf16[1,512,3,4,256]{4,1,2,0,3:T(8,128)(2,1)}, u32[]{:S(2)}, u32[]{:S(2)}) %all-to-all-start) | async-done | bytes 3145760 | tf_op jit(solution)/shard_map/all_to_all | solution.py:183
  72.1 6.2 copy.64
  78.3 6.1 reshape.606
  91.1 90.9 %while.46 = (s32[]{:T(128)}, bf16[4,512,4,64]{1,3,2,0:T(8,128)(2,1)}, f32[4,4,512]{2,1,0:T(4,128)S(1)}, s32[4,512]{1,0:T(4,128)S(1)}, s32[2048]{0:T(1024)S(1)}, ...) while((s32[]{:T(128)}, ...), condition=%wide.region_5.6_spmd.clone, body=%wide.region_2.5_spmd.clone.sunk | while | flops 1152516096 | bytes 99192080 | solution.py:75
  93.9 6.3 fusion.125
  100.2 5.8 exponential_reduce_fusion.2
  106.0 8.2 fusion.126
  116.5 6.3 fusion.125
  122.8 5.8 exponential_reduce_fusion.2
  128.6 8.2 fusion.126
  139.1 6.3 fusion.125
  145.4 5.8 exponential_reduce_fusion.2
  151.2 8.2 fusion.126
  161.7 6.3 fusion.125
  168.0 5.8 exponential_reduce_fusion.2
  173.8 8.2 fusion.126
  186.1 8.2 reshape.615
  194.8 11.8 reduce.26
  212.7 13.6 %all-to-all-done.1 = bf16[4,2,65536]{2,1,0:T(2,128)(2,1)S(1)} async-done(((bf16[4,2,65536]{2,1,0:T(2,128)(2,1)}), bf16[4,2,65536]{2,1,0:T(2,128)(2,1)S(1)}, u32[]{:S(2)}, u32[]{:S(2)}) %all-to-all-start.1) | async-done | bytes 1048608 | tf_op jit(solution)/shard_map/all_to_all | solution.py:191
  236.2 27.8 %multiply_convert_fusion.1 = (bf16[512,4096]{1,0:T(8,128)(2,1)}, f32[512,4096]{1,0:T(8,128)}, f32[512,4096]{1,0:T(8,128)}) fusion(f32[4096]{0:T(1024)S(1)} %convert_element_type.104, bf16[1024,4096]{1,0:T(8,128)(2,1)} %param.27, f32[512,1024]{1,0:T(8,128)S(1)} %get-tuple-element.449, f32[1024]{0:T(1024)S(1)} %convert_element_type.102, ...), kind=kOutput, calls=%fused_computation.65 | convolution fusion | flops 4435476480 | bytes 31481856 | tf_op jit(solution)/shard_map/rfd,dk->rfk/dot_general | solution.py:198
  264.0 14.0 %convert_reduce_fusion = (f32[4096]{0:T(1024)}, bf16[512,4096]{1,0:T(8,128)(2,1)S(1)}) fusion(f32[512,4096]{1,0:T(8,128)} %get-tuple-element.430, bf16[4096,1024]{1,0:T(8,128)(2,1)} %param.29, bf16[1,512,1024]{2,1,0:T(8,128)(2,1)S(1)} %copy-done.18, f32[512,4096]{1,0:T(8,128)} %get-tuple-element.450, f32[4096]{0:T(1024)S(1)} %convert_element_type.104), kind=kOutput, calls=%fused_computation.63 | convolution fusion | flops 4330614784 | bytes 30441472 | tf_op jit(solution)/shard_map/rfd,kd->rfk/dot_general | solution.py:210
  278.0 9.6 multiply_reduce_fusion.1
  297.8 5.1 all-to-all-start.2
  306.2 11.3 all-to-all-done.2
  319.7 236.1 %while.47 = (s32[]{:T(128)}, f32[2048,4,64]{0,2,1:T(8,128)}, f32[2048,4,64]{0,2,1:T(8,128)}, bf16[4,512,4,64]{1,3,2,0:T(8,128)(2,1)}, bf16[4,512,4,64]{1,3,2,0:T...) while((s32[]{:T(128)}, f32[2048,4,64]{0,2,1:T(8,128)}, ...), condition=%wide.region_12.13_spmd.clone, body=%wide.region_10.12_spmd.clone.sunk | while | flops 2740584448 | bytes 224997680 | solution.py:131
  321.2 9.1 fusion.136
  331.1 14.0 %multiply_reduce_fusion.10 = (f32[4,512]{1,0:T(4,128)S(1)}, f32[4,512,2048]{2,1,0:T(8,128)}) fusion(f32[4,512,2048]{2,1,0:T(8,128)} %fusion.136, f32[4,512]{1,0:T(4,128)S(1)} %dynamic-slice_bitcast_fusion.2, f32[512,2048]{1,0:T(8,128)S(1)} %abs_convert_fusion.5, f32[4]{0:T(128)S(1)} %multiply_exponential_fusion.5, ...), kind=kOutput, calls=%fused_computation.27.clone.1 | convolution fusion | flops 566228992 | bytes 40124944 | tf_op jit(solution)/shard_map/while/body/eval_jaxpr/while/body/eval_jaxpr/qhd,khd->hqk/dot_general | solution.py:39
  345.1 15.2 %multiply_convert_fusion.9 = bf16[4,512,2048]{2,1,0:T(8,128)(2,1)} fusion(f32[4,512,2048]{2,1,0:T(8,128)} %get-tuple-element.627, f32[4,512,2048]{2,1,0:T(8,128)} %fusion.136, f32[4,512]{1,0:T(4,128)S(1)} %get-tuple-element.628), kind=kLoop, calls=%fused_computation.26.clone.1 | loop fusion | flops 12582912 | bytes 41951232 | tf_op jit(solution)/shard_map/while/body/eval_jaxpr/while/body/eval_jaxpr/convert_element_type | solution.py:118
  360.2 6.6 fusion.138
  366.8 6.8 fusion.140
  379.3 9.1 fusion.136
  389.1 14.0 %multiply_reduce_fusion.10 = (f32[4,512]{1,0:T(4,128)S(1)}, f32[4,512,2048]{2,1,0:T(8,128)}) fusion(f32[4,512,2048]{2,1,0:T(8,128)} %fusion.136, f32[4,512]{1,0:T(4,128)S(1)} %dynamic-slice_bitcast_fusion.2, f32[512,2048]{1,0:T(8,128)S(1)} %abs_convert_fusion.5, f32[4]{0:T(128)S(1)} %multiply_exponential_fusion.5, ...), kind=kOutput, calls=%fused_computation.27.clone.1 | convolution fusion | flops 566228992 | bytes 40124944 | tf_op jit(solution)/shard_map/while/body/eval_jaxpr/while/body/eval_jaxpr/qhd,khd->hqk/dot_general | solution.py:39
  403.1 15.1 %multiply_convert_fusion.9 = bf16[4,512,2048]{2,1,0:T(8,128)(2,1)} fusion(f32[4,512,2048]{2,1,0:T(8,128)} %get-tuple-element.627, f32[4,512,2048]{2,1,0:T(8,128)} %fusion.136, f32[4,512]{1,0:T(4,128)S(1)} %get-tuple-element.628), kind=kLoop, calls=%fused_computation.26.clone.1 | loop fusion | flops 12582912 | bytes 41951232 | tf_op jit(solution)/shard_map/while/body/eval_jaxpr/while/body/eval_jaxpr/convert_element_type | solution.py:118
  418.2 7.2 fusion.138
  425.4 6.8 fusion.140
  432.2 5.0 fusion.139
  438.7 9.1 fusion.136
  448.6 13.9 %multiply_reduce_fusion.10 = (f32[4,512]{1,0:T(4,128)S(1)}, f32[4,512,2048]{2,1,0:T(8,128)}) fusion(f32[4,512,2048]{2,1,0:T(8,128)} %fusion.136, f32[4,512]{1,0:T(4,128)S(1)} %dynamic-slice_bitcast_fusion.2, f32[512,2048]{1,0:T(8,128)S(1)} %abs_convert_fusion.5, f32[4]{0:T(128)S(1)} %multiply_exponential_fusion.5, ...), kind=kOutput, calls=%fused_computation.27.clone.1 | convolution fusion | flops 566228992 | bytes 40124944 | tf_op jit(solution)/shard_map/while/body/eval_jaxpr/while/body/eval_jaxpr/qhd,khd->hqk/dot_general | solution.py:39
  462.5 15.0 %multiply_convert_fusion.9 = bf16[4,512,2048]{2,1,0:T(8,128)(2,1)} fusion(f32[4,512,2048]{2,1,0:T(8,128)} %get-tuple-element.627, f32[4,512,2048]{2,1,0:T(8,128)} %fusion.136, f32[4,512]{1,0:T(4,128)S(1)} %get-tuple-element.628), kind=kLoop, calls=%fused_computation.26.clone.1 | loop fusion | flops 12582912 | bytes 41951232 | tf_op jit(solution)/shard_map/while/body/eval_jaxpr/while/body/eval_jaxpr/convert_element_type | solution.py:118
  477.5 7.2 fusion.138
  484.6 6.8 fusion.140
  497.9 9.1 fusion.136
  507.8 13.9 %multiply_reduce_fusion.10 = (f32[4,512]{1,0:T(4,128)S(1)}, f32[4,512,2048]{2,1,0:T(8,128)}) fusion(f32[4,512,2048]{2,1,0:T(8,128)} %fusion.136, f32[4,512]{1,0:T(4,128)S(1)} %dynamic-slice_bitcast_fusion.2, f32[512,2048]{1,0:T(8,128)S(1)} %abs_convert_fusion.5, f32[4]{0:T(128)S(1)} %multiply_exponential_fusion.5, ...), kind=kOutput, calls=%fused_computation.27.clone.1 | convolution fusion | flops 566228992 | bytes 40124944 | tf_op jit(solution)/shard_map/while/body/eval_jaxpr/while/body/eval_jaxpr/qhd,khd->hqk/dot_general | solution.py:39
  521.7 15.0 %multiply_convert_fusion.9 = bf16[4,512,2048]{2,1,0:T(8,128)(2,1)} fusion(f32[4,512,2048]{2,1,0:T(8,128)} %get-tuple-element.627, f32[4,512,2048]{2,1,0:T(8,128)} %fusion.136, f32[4,512]{1,0:T(4,128)S(1)} %get-tuple-element.628), kind=kLoop, calls=%fused_computation.26.clone.1 | loop fusion | flops 12582912 | bytes 41951232 | tf_op jit(solution)/shard_map/while/body/eval_jaxpr/while/body/eval_jaxpr/convert_element_type | solution.py:118
  536.7 7.2 fusion.138
  543.9 6.8 fusion.140
  550.7 5.0 fusion.139
  563.7 7.2 copy.73
  570.8 52.3 %all_to_all.60 = bf16[1,2048,3,1,256]{4,2,3,0,1:T(4,128)(2,1)S(1)} all-to-all(bf16[1,2048,3,1,256]{4,2,3,0,1:T(4,128)(2,1)} %copy.73), channel_id=1, replica_groups=mesh['rows'=8,'seq'=4] {'seq'}, dimensions={1} | all-to-all | bytes 6291456 | tf_op jit(solution)/shard_map/all_to_all | solution.py:244
  630.0 8.6 fusion.69
  638.7 8.6 multiply_reduce_fusion.2
  649.1 5.7 fusion.53
  656.5 11.3 fusion.70
  669.1 11.1 fusion.59
  680.9 10.8 fusion.52
  691.8 43.6 %all-reduce.4 = (f32[1024]{0:T(1024)S(1)}, f32[1024]{0:T(1024)S(1)}, f32[4096]{0:T(1024)S(1)}, f32[1024]{0:T(1024)S(1)}) all-reduce(f32[1024]{0:T(1024)S(1)} %get-tuple-element.369, f32[1024]{0:T(1024)S(1)} %copy-done.41, f32[4096]{0:T(1024)S(1)} %copy-done.35, ...), channel_id=3, replica_groups=mesh['rows'=8,'seq'=4] {'rows','seq'}, use_global_device_ids=true, to_apply=%region_17.18.clone | all-reduce | flops 7168 | bytes 57344
  743.9 50.7 %reduce-scatter.8.cloned.1.call-done = f32[32,3072]{1,0:T(8,128)} async-done(((f32[1024,3072]{1,0:T(8,128)}), f32[32,3072]{1,0:T(8,128)}) %reduce-scatter.8.cloned.1.call-update) | async-done | bytes 393232 | tf_op jit(solution)/shard_map/reduce_scatter | solution.py:267
  794.7 139.3 %reduce-scatter.6.cloned.1.call-done = f32[64,1024]{1,0:T(8,128)} async-done(((f32[2048,1024]{1,0:T(8,128)}), f32[64,1024]{1,0:T(8,128)}) %reduce-scatter.6.cloned.1.call-update) | async-done | bytes 262160 | tf_op jit(solution)/shard_map/reduce_scatter | solution.py:265
  934.0 197.1 %reduce-scatter.12.cloned.1.call-done = f32[32,4096]{1,0:T(8,128)} async-done(((f32[1024,4096]{1,0:T(8,128)}), f32[32,4096]{1,0:T(8,128)}) %reduce-scatter.12.cloned.1.call-update) | async-done | bytes 524304 | tf_op jit(solution)/shard_map/reduce_scatter | solution.py:270
  1131.1 188.2 %reduce-scatter.14.cloned.1.call-done = f32[128,1024]{1,0:T(8,128)} async-done(((f32[4096,1024]{1,0:T(8,128)}), f32[128,1024]{1,0:T(8,128)}) %reduce-scatter.14.cloned.1.call-update) | async-done | bytes 524304 | tf_op jit(solution)/shard_map/reduce_scatter | solution.py:272
  (249 shorter events, 106.1 us)
Async XLA Ops:
  7.2 225.6 %copy-start = (bf16[1024,1024]{1,0:T(8,128)(2,1)S(1)}, bf16[1024,1024]{1,0:T(8,128)(2,1)}, u32[]{:S(2)}) copy-start(bf16[1024,1024]{1,0:T(8,128)(2,1)} %param.25) | copy-start | bytes 6291460
  7.2 5.8 copy-start.42
  7.2 7.4 copy-start.45
  30.5 5.9 copy-start.24
  30.5 41.6 %all-to-all-start = ((bf16[1,512,3,4,256]{4,1,2,0,3:T(8,128)(2,1)}), bf16[1,512,3,4,256]{4,1,2,0,3:T(8,128)(2,1)}, u32[]{:S(2)}, u32[]{:S(2)}) async-start(bf16[1,512,3,4,256]{4,1,2,0,3:T(8,128)(2,1)} %copy.63), calls=%async_computation | async-start | bytes 6291456 | tf_op jit(solution)/shard_map/all_to_all | solution.py:183
  84.4 6.7 copy-start.25
  91.6 2.3 copy-start.4
  93.1 7.1 copy-start.6
  93.8 6.3 copy-start.3
  114.2 2.3 copy-start.4
  115.7 7.1 copy-start.6
  116.4 6.3 copy-start.3
  136.8 2.3 copy-start.4
  138.3 7.1 copy-start.6
  139.0 6.3 copy-start.3
  159.4 2.3 copy-start.4
  160.9 7.1 copy-start.6
  161.6 6.3 copy-start.3
  194.3 18.3 %copy-start.43 = (bf16[1024]{0:T(1024)(128)(2,1)S(1)}, bf16[1024]{0:T(1024)(128)(2,1)}, u32[]{:S(2)}) copy-start(bf16[1024]{0:T(1024)(128)(2,1)} %param.26) | copy-start | bytes 6148
  194.3 18.3 %copy-start.38 = (bf16[4096]{0:T(1024)(128)(2,1)S(1)}, bf16[4096]{0:T(1024)(128)(2,1)}, u32[]{:S(2)}) copy-start(bf16[4096]{0:T(1024)(128)(2,1)} %param.28) | copy-start | bytes 24580
  208.3 17.9 %all-to-all-start.1 = ((bf16[4,2,65536]{2,1,0:T(2,128)(2,1)}), bf16[4,2,65536]{2,1,0:T(2,128)(2,1)S(1)}, u32[]{:S(2)}, u32[]{:S(2)}) async-start(bf16[4,2,65536]{2,1,0:T(2,128)(2,1)} %reshape.628), calls=%async_computation.1 | async-start | bytes 2097152 | tf_op jit(solution)/shard_map/all_to_all | solution.py:191
  212.7 74.9 %copy-start.31 = (f32[1024]{0:T(1024)}, f32[1024]{0:T(1024)S(1)}, u32[]{:S(2)}) copy-start(f32[1024]{0:T(1024)S(1)} %convert_element_type.102) | copy-start | bytes 12292
  235.8 51.8 %copy-start.12 = (f32[512,1024]{1,0:T(8,128)}, f32[512,1024]{1,0:T(8,128)S(1)}, u32[]{:S(2)}) copy-start(f32[512,1024]{1,0:T(8,128)S(1)} %get-tuple-element.449) | copy-start | bytes 6291460
  235.8 51.8 %copy-start.26 = (f32[512]{0:T(512)}, f32[512]{0:T(512)S(1)}, u32[]{:S(2)}) copy-start(f32[512]{0:T(512)S(1)} %broadcast_multiply_fusion.4) | copy-start | bytes 6148
  236.1 51.4 %copy-start.36 = (f32[512]{0:T(512)}, f32[512]{0:T(512)S(1)}, u32[]{:S(2)}) copy-start(f32[512]{0:T(512)S(1)} %add_rsqrt_fusion) | copy-start | bytes 6148
  236.1 27.8 %copy-start.18 = (bf16[1,512,1024]{2,1,0:T(8,128)(2,1)S(1)}, bf16[1,512,1024]{2,1,0:T(8,128)(2,1)}, u32[]{:S(2)}) copy-start(bf16[1,512,1024]{2,1,0:T(8,128)(2,1)} %param.31) | copy-start | bytes 3145732
  278.0 9.6 copy-start.48
  292.6 10.2 copy-start.10
  297.8 19.7 %all-to-all-start.2 = ((bf16[1,512,4,256]{3,1,0,2:T(8,128)(2,1)}), bf16[1,512,4,256]{3,1,0,2:T(8,128)(2,1)}, u32[]{:S(2)}, u32[]{:S(2)}) async-start(bf16[1,512,4,256]{3,1,0,2:T(8,128)(2,1)} %copy.69), calls=%async_computation.2 | async-start | bytes 2097152 | tf_op jit(solution)/shard_map/all_to_all | solution.py:222
  302.9 441.1 %reduce-scatter.10.cloned.1.call-start = ((), (), s32[]{:S(2)}) async-start(), calls=%async_computation.11 | async-start | bytes 4325376 | tf_op jit(solution)/shard_map/reduce_scatter | solution.py:268
  306.1 13.6 %copy-start.5 = (bf16[2048,4,64]{0,2,1:T(8,128)(2,1)S(1)}, bf16[2048,4,64]{0,2,1:T(8,128)(2,1)}, u32[]{:S(2)}) copy-start(bf16[2048,4,64]{0,2,1:T(8,128)(2,1)} %get-tuple-element.718) | copy-start | bytes 3145732
  306.1 13.6 %copy-start.8 = (bf16[2048,4,64]{0,2,1:T(8,128)(2,1)S(1)}, bf16[2048,4,64]{0,2,1:T(8,128)(2,1)}, u32[]{:S(2)}) copy-start(bf16[2048,4,64]{0,2,1:T(8,128)(2,1)} %get-tuple-element.719) | copy-start | bytes 3145732
  306.1 488.5 %reduce-scatter.8.cloned.1.call-start = ((), (), s32[]{:S(2)}) async-start(), calls=%async_computation.10 | async-start | bytes 12976128 | tf_op jit(solution)/shard_map/reduce_scatter | solution.py:267
  345.1 21.8 %copy-start.20 = (bf16[4,512,4,64]{1,3,2,0:T(8,128)(2,1)S(1)}, bf16[4,512,4,64]{1,3,2,0:T(8,128)(2,1)}, u32[]{:S(2)}) copy-start(bf16[4,512,4,64]{1,3,2,0:T(8,128)(2,1)} %get-tuple-element.684) | copy-start | bytes 3145732 | tf_op jit(solution)/shard_map/while/body/eval_jaxpr/while
  360.2 13.4 %copy-start.2 = (f32[4,512,2048]{2,1,0:T(8,128)S(1)}, f32[4,512,2048]{2,1,0:T(8,128)}, u32[]{:S(2)}) copy-start(f32[4,512,2048]{2,1,0:T(8,128)} %get-tuple-element.627) | copy-start | bytes 50331652 | tf_op jit(solution)/shard_map/while/body/eval_jaxpr/while
  373.6 4.1 copy-start.21
  403.1 22.3 %copy-start.20 = (bf16[4,512,4,64]{1,3,2,0:T(8,128)(2,1)S(1)}, bf16[4,512,4,64]{1,3,2,0:T(8,128)(2,1)}, u32[]{:S(2)}) copy-start(bf16[4,512,4,64]{1,3,2,0:T(8,128)(2,1)} %get-tuple-element.684) | copy-start | bytes 3145732 | tf_op jit(solution)/shard_map/while/body/eval_jaxpr/while
  418.2 14.0 %copy-start.2 = (f32[4,512,2048]{2,1,0:T(8,128)S(1)}, f32[4,512,2048]{2,1,0:T(8,128)}, u32[]{:S(2)}) copy-start(f32[4,512,2048]{2,1,0:T(8,128)} %get-tuple-element.627) | copy-start | bytes 50331652 | tf_op jit(solution)/shard_map/while/body/eval_jaxpr/while
  432.2 5.0 copy-start.21
  462.5 22.2 %copy-start.20 = (bf16[4,512,4,64]{1,3,2,0:T(8,128)(2,1)S(1)}, bf16[4,512,4,64]{1,3,2,0:T(8,128)(2,1)}, u32[]{:S(2)}) copy-start(bf16[4,512,4,64]{1,3,2,0:T(8,128)(2,1)} %get-tuple-element.684) | copy-start | bytes 3145732 | tf_op jit(solution)/shard_map/while/body/eval_jaxpr/while
  477.5 14.0 %copy-start.2 = (f32[4,512,2048]{2,1,0:T(8,128)S(1)}, f32[4,512,2048]{2,1,0:T(8,128)}, u32[]{:S(2)}) copy-start(f32[4,512,2048]{2,1,0:T(8,128)} %get-tuple-element.627) | copy-start | bytes 50331652 | tf_op jit(solution)/shard_map/while/body/eval_jaxpr/while
  491.4 5.0 copy-start.21
  521.7 22.2 %copy-start.20 = (bf16[4,512,4,64]{1,3,2,0:T(8,128)(2,1)S(1)}, bf16[4,512,4,64]{1,3,2,0:T(8,128)(2,1)}, u32[]{:S(2)}) copy-start(bf16[4,512,4,64]{1,3,2,0:T(8,128)(2,1)} %get-tuple-element.684) | copy-start | bytes 3145732 | tf_op jit(solution)/shard_map/while/body/eval_jaxpr/while
  536.7 14.0 %copy-start.2 = (f32[4,512,2048]{2,1,0:T(8,128)S(1)}, f32[4,512,2048]{2,1,0:T(8,128)}, u32[]{:S(2)}) copy-start(f32[4,512,2048]{2,1,0:T(8,128)} %get-tuple-element.627) | copy-start | bytes 50331652 | tf_op jit(solution)/shard_map/while/body/eval_jaxpr/while
  550.7 5.0 copy-start.21
  555.8 3.8 copy-start.7
  559.6 2.0 copy-start.17
  625.1 4.8 copy-start.15
  625.1 4.8 copy-start.29
  625.1 4.9 copy-start.34
  625.1 4.9 copy-start.40
  638.6 8.7 copy-start.11
  638.7 295.3 %reduce-scatter.6.cloned.1.call-start = ((), (), s32[]{:S(2)}) async-start(), calls=%async_computation.9 | async-start | bytes 8650752 | tf_op jit(solution)/shard_map/reduce_scatter | solution.py:265
  638.7 8.7 copy-start.16
  647.3 1.8 copy-start.46
  647.3 1.8 copy-start.47
  654.8 1.7 copy-start.37
  654.8 476.3 %reduce-scatter.12.cloned.1.call-start = ((), (), s32[]{:S(2)}) async-start(), calls=%async_computation.12 | async-start | bytes 17301504 | tf_op jit(solution)/shard_map/reduce_scatter | solution.py:270
  667.8 651.5 %reduce-scatter.14.cloned.1.call-start = ((), (), s32[]{:S(2)}) async-start(), calls=%async_computation.13 | async-start | bytes 17301504 | tf_op jit(solution)/shard_map/reduce_scatter | solution.py:272
  680.9 10.9 copy-start.30
  680.9 10.9 copy-start.35
  680.9 10.9 copy-start.41
  680.9 56.8 %copy-start.23 = (bf16[512,1024]{1,0:T(8,128)(2,1)S(1)}, bf16[512,1024]{1,0:T(8,128)(2,1)}, u32[]{:S(2)}) copy-start(bf16[512,1024]{1,0:T(8,128)(2,1)} %copy-done.22) | copy-start | bytes 3145732
  737.7 581.6 %copy-start.1 = (bf16[1024,1024]{1,0:T(8,128)(2,1)S(1)}, bf16[1024,1024]{1,0:T(8,128)(2,1)}, u32[]{:S(2)}) copy-start(bf16[1024,1024]{1,0:T(8,128)(2,1)} %param.25) | copy-start | bytes 6291460
  (11 other events, 13.8 us)
Sparse Core Ops, SparseCore 0:
  306.5 126.9 reduce-scatter.9
  638.8 155.8 reduce-scatter.7
  797.6 136.2 reduce-scatter.5
  936.8 194.2 reduce-scatter.11
  1133.9 185.3 reduce-scatter.13
where the time goes:
time: 1330 us
  waiting for transfers between devices  635 us (48%)
  matrix products  355 us (27%)
  other arithmetic  121 us (9%)
  blocking collectives  95.9 us (7%)
  local copies, waits for them, and re-layouts  87.9 us (7%)
  starting transfers between devices  15.2 us (1%)
  between operations  14.4 us (1%)
    reduce_scatter x1, waiting for transfers between devices, body(): lax.psum_scatter(up_grad, ('rows', 'seq'), scatter_dimension=0, tiled=True)  197 us
    reduce_scatter x1, waiting for transfers between devices, body(): lax.psum_scatter(down_grad, ('rows', 'seq'), scatter_dimension=0, tiled=T...  188 us
    reduce_scatter x1, waiting for transfers between devices, body(): lax.psum_scatter(skip_w_grad, ('rows', 'seq'), scatter_dimension=0, tiled...  139 us
    dot_general x8, matrix products, block_scores(): jnp.einsum('qhd,khd->hqk', q_blk, all_keys, preferred_element_type=jnp.fl...  80.9 us
    convert_element_type x4, other arithmetic, one_block(): score_grad = (soft * (prob_grad - jnp.sum(soft * prob_grad, axis=-1, keep...  60.2 us
    all_to_all x1, blocking collectives, body(): lax.all_to_all(packed_grad, 'seq', split_axis=1, concat_axis=3, tiled=True)  52.3 us
    reduce_scatter x1, waiting for transfers between devices, body(): lax.psum_scatter(qkv_grad, ('rows', 'seq'), scatter_dimension=0, tiled=True)  50.7 us
    unnamed x1, blocking collectives  43.6 us
  transfers between devices with their start and end apart: 8, of which 7 were waited for; matrix products, arithmetic and copies ran while one was open for 25% of the time, Pallas kernels for 0%

commit v1 on v0

--- a/solution.py
+++ b/solution.py
@@ -241,7 +241,9 @@
         )
 
     packed_grad = lax.map(backward_row, (by_heads, log_total, grad_heads, seg_ids, frame_valid))
-    packed_back = lax.all_to_all(packed_grad, "seq", split_axis=1, concat_axis=3, tiled=True)
+    pieces = jnp.split(packed_grad, lax.axis_size("seq"), axis=1)
+    got = lax.all_to_all(jnp.stack(pieces), "seq", 0, 0)
+    packed_back = jnp.concatenate(got, axis=3)
     packed_back = packed_back.reshape(rows_here, frames, 3 * D)
     qkv_grad = jnp.einsum("rfd,rfe->de", normed, packed_back, preferred_element_type=jnp.float32)
     normed_grad = jnp.einsum("rfe,de->rfd", packed_back, w_qkv, preferred_element_type=jnp.float32)

time: 1330 us -> 1310 us (0.985)
  transfers between devices with their start and end apart: 8 -> 8, of which waited for: 7 -> 7; matrix products, arithmetic and copies ran while one was open for 25% -> 24% of each run, Pallas kernels for 0% -> 0%
where the time goes in v1:
time: 1310 us; the launch traced here: 1300 us
  waiting for transfers between devices  634 us (48%)
  matrix products  354 us (27%)
  other arithmetic  120 us (9%)
  blocking collectives  83.3 us (6%)
  local copies, waits for them, and re-layouts  77.9 us (6%)
  starting transfers between devices  15 us (1%)
  between operations  14.5 us (1%)
    reduce_scatter x1, waiting for transfers between devices, body(): lax.psum_scatter(up_grad, ('rows', 'seq'), scatter_dimension=0, tiled=True)  199 us
    reduce_scatter x1, waiting for transfers between devices, body(): lax.psum_scatter(down_grad, ('rows', 'seq'), scatter_dimension=0, tiled=T...  187 us
    reduce_scatter x1, waiting for transfers between devices, body(): lax.psum_scatter(skip_w_grad, ('rows', 'seq'), scatter_dimension=0, tiled...  138 us
    dot_general x8, matrix products, block_scores(): jnp.einsum('qhd,khd->hqk', q_blk, all_keys, preferred_element_type=jnp.fl...  80.8 us
    convert_element_type x4, other arithmetic, one_block(): score_grad = (soft * (prob_grad - jnp.sum(soft * prob_grad, axis=-1, keep...  60.2 us
    reduce_scatter x1, waiting for transfers between devices, body(): lax.psum_scatter(qkv_grad, ('rows', 'seq'), scatter_dimension=0, tiled=True)  50.7 us
    unnamed x1, blocking collectives  43.5 us
    all_to_all x1, blocking collectives, body(): got = lax.all_to_all(jnp.stack(pieces), 'seq', 0, 0)  39.8 us
  transfers between devices with their start and end apart: 8, of which 7 were waited for; matrix products, arithmetic and copies ran while one was open for 24% of the time, Pallas kernels for 0%

profile of v1, /device:TPU:3, one launch (start us, length us, event | category | flops | bytes accessed | tf_op | source)
XLA Modules:
  0.0 1299.4 jit_solution(10385991138284285976)
XLA Ops:
  7.2 5.4 fusion.75
  14.5 5.3 convolution_convert_fusion
  19.8 6.7 reshape.606
  30.5 5.4 all-to-all-start
  37.1 35.0 %all-to-all-done = bf16[1,512,3,4,256]{4,1,2,0,3:T(8,128)(2,1)} async-done(((bf16[1,512,3,4,256]{4,1,2,0,3:T(8,128)(2,1)}), bf16[1,512,3,4,256]{4,1,2,0,3:T(8,128)(2,1)}, u32[]{:S(2)}, u32[]{:S(2)}) %all-to-all-start) | async-done | bytes 3145760 | tf_op jit(solution)/shard_map/all_to_all | solution.py:183
  72.0 6.2 copy.74
  78.2 6.1 reshape.607
  91.1 90.9 %while.46 = (s32[]{:T(128)}, bf16[4,512,4,64]{1,3,2,0:T(8,128)(2,1)}, f32[4,4,512]{2,1,0:T(4,128)S(1)}, s32[4,512]{1,0:T(4,128)S(1)}, s32[2048]{0:T(1024)S(1)}, ...) while((s32[]{:T(128)}, ...), condition=%wide.region_5.6_spmd.clone, body=%wide.region_2.5_spmd.clone.sunk | while | flops 1152516096 | bytes 99192080 | solution.py:75
  93.8 6.3 fusion.126
  100.1 5.8 exponential_reduce_fusion.2
  106.0 8.1 fusion.127
  116.4 6.3 fusion.126
  122.7 5.8 exponential_reduce_fusion.2
  128.6 8.2 fusion.127
  139.0 6.3 fusion.126
  145.3 5.8 exponential_reduce_fusion.2
  151.2 8.2 fusion.127
  161.6 6.3 fusion.126
  167.9 5.8 exponential_reduce_fusion.2
  173.8 8.2 fusion.127
  186.0 8.2 reshape.617
  194.7 11.8 reduce.26
  212.6 13.6 %all-to-all-done.1 = bf16[4,2,65536]{2,1,0:T(2,128)(2,1)S(1)} async-done(((bf16[4,2,65536]{2,1,0:T(2,128)(2,1)}), bf16[4,2,65536]{2,1,0:T(2,128)(2,1)S(1)}, u32[]{:S(2)}, u32[]{:S(2)}) %all-to-all-start.1) | async-done | bytes 1048608 | tf_op jit(solution)/shard_map/all_to_all | solution.py:191
  236.1 27.8 %multiply_convert_fusion.1 = (bf16[512,4096]{1,0:T(8,128)(2,1)}, f32[512,4096]{1,0:T(8,128)}, f32[512,4096]{1,0:T(8,128)}) fusion(f32[4096]{0:T(1024)S(1)} %convert_element_type.104, bf16[1024,4096]{1,0:T(8,128)(2,1)} %param.27, f32[512,1024]{1,0:T(8,128)S(1)} %get-tuple-element.454, f32[1024]{0:T(1024)S(1)} %convert_element_type.102, ...), kind=kOutput, calls=%fused_computation.65 | convolution fusion | flops 4435476480 | bytes 31481856 | tf_op jit(solution)/shard_map/rfd,dk->rfk/dot_general | solution.py:198
  263.9 14.0 %convert_reduce_fusion = (f32[4096]{0:T(1024)}, bf16[512,4096]{1,0:T(8,128)(2,1)S(1)}) fusion(f32[512,4096]{1,0:T(8,128)} %get-tuple-element.430, bf16[4096,1024]{1,0:T(8,128)(2,1)} %param.29, bf16[1,512,1024]{2,1,0:T(8,128)(2,1)S(1)} %copy-done.18, f32[512,4096]{1,0:T(8,128)} %get-tuple-element.455, f32[4096]{0:T(1024)S(1)} %convert_element_type.104), kind=kOutput, calls=%fused_computation.63 | convolution fusion | flops 4330614784 | bytes 30441472 | tf_op jit(solution)/shard_map/rfd,kd->rfk/dot_general | solution.py:210
  277.9 9.5 multiply_reduce_fusion.1
  297.6 5.1 all-to-all-start.2
  306.0 11.3 all-to-all-done.2
  319.6 235.9 %while.47 = (s32[]{:T(128)}, f32[2048,4,64]{0,2,1:T(8,128)}, f32[2048,4,64]{0,2,1:T(8,128)}, bf16[4,512,4,64]{1,3,2,0:T(8,128)(2,1)}, bf16[4,512,4,64]{1,3,2,0:T...) while((s32[]{:T(128)}, f32[2048,4,64]{0,2,1:T(8,128)}, ...), condition=%wide.region_12.13_spmd.clone, body=%wide.region_10.12_spmd.clone.sunk | while | flops 2740584448 | bytes 224997680 | solution.py:131
  321.1 9.1 fusion.137
  330.9 14.0 %multiply_reduce_fusion.10 = (f32[4,512]{1,0:T(4,128)S(1)}, f32[4,512,2048]{2,1,0:T(8,128)}) fusion(f32[4,512,2048]{2,1,0:T(8,128)} %fusion.137, f32[4,512]{1,0:T(4,128)S(1)} %dynamic-slice_bitcast_fusion.2, f32[512,2048]{1,0:T(8,128)S(1)} %abs_convert_fusion.5, f32[4]{0:T(128)S(1)} %multiply_exponential_fusion.5, ...), kind=kOutput, calls=%fused_computation.27.clone.1 | convolution fusion | flops 566228992 | bytes 40124944 | tf_op jit(solution)/shard_map/while/body/eval_jaxpr/while/body/eval_jaxpr/qhd,khd->hqk/dot_general | solution.py:39
  344.9 15.2 %multiply_convert_fusion.9 = bf16[4,512,2048]{2,1,0:T(8,128)(2,1)} fusion(f32[4,512,2048]{2,1,0:T(8,128)} %get-tuple-element.632, f32[4,512,2048]{2,1,0:T(8,128)} %fusion.137, f32[4,512]{1,0:T(4,128)S(1)} %get-tuple-element.633), kind=kLoop, calls=%fused_computation.26.clone.1 | loop fusion | flops 12582912 | bytes 41951232 | tf_op jit(solution)/shard_map/while/body/eval_jaxpr/while/body/eval_jaxpr/convert_element_type | solution.py:118
  360.0 6.6 fusion.139
  366.6 6.8 fusion.141
  379.1 9.1 fusion.137
  388.9 14.0 %multiply_reduce_fusion.10 = (f32[4,512]{1,0:T(4,128)S(1)}, f32[4,512,2048]{2,1,0:T(8,128)}) fusion(f32[4,512,2048]{2,1,0:T(8,128)} %fusion.137, f32[4,512]{1,0:T(4,128)S(1)} %dynamic-slice_bitcast_fusion.2, f32[512,2048]{1,0:T(8,128)S(1)} %abs_convert_fusion.5, f32[4]{0:T(128)S(1)} %multiply_exponential_fusion.5, ...), kind=kOutput, calls=%fused_computation.27.clone.1 | convolution fusion | flops 566228992 | bytes 40124944 | tf_op jit(solution)/shard_map/while/body/eval_jaxpr/while/body/eval_jaxpr/qhd,khd->hqk/dot_general | solution.py:39
  402.9 15.1 %multiply_convert_fusion.9 = bf16[4,512,2048]{2,1,0:T(8,128)(2,1)} fusion(f32[4,512,2048]{2,1,0:T(8,128)} %get-tuple-element.632, f32[4,512,2048]{2,1,0:T(8,128)} %fusion.137, f32[4,512]{1,0:T(4,128)S(1)} %get-tuple-element.633), kind=kLoop, calls=%fused_computation.26.clone.1 | loop fusion | flops 12582912 | bytes 41951232 | tf_op jit(solution)/shard_map/while/body/eval_jaxpr/while/body/eval_jaxpr/convert_element_type | solution.py:118
  417.9 7.2 fusion.139
  425.1 6.8 fusion.141
  431.9 5.0 fusion.140
  438.4 9.1 fusion.137
  448.3 13.9 %multiply_reduce_fusion.10 = (f32[4,512]{1,0:T(4,128)S(1)}, f32[4,512,2048]{2,1,0:T(8,128)}) fusion(f32[4,512,2048]{2,1,0:T(8,128)} %fusion.137, f32[4,512]{1,0:T(4,128)S(1)} %dynamic-slice_bitcast_fusion.2, f32[512,2048]{1,0:T(8,128)S(1)} %abs_convert_fusion.5, f32[4]{0:T(128)S(1)} %multiply_exponential_fusion.5, ...), kind=kOutput, calls=%fused_computation.27.clone.1 | convolution fusion | flops 566228992 | bytes 40124944 | tf_op jit(solution)/shard_map/while/body/eval_jaxpr/while/body/eval_jaxpr/qhd,khd->hqk/dot_general | solution.py:39
  462.2 15.0 %multiply_convert_fusion.9 = bf16[4,512,2048]{2,1,0:T(8,128)(2,1)} fusion(f32[4,512,2048]{2,1,0:T(8,128)} %get-tuple-element.632, f32[4,512,2048]{2,1,0:T(8,128)} %fusion.137, f32[4,512]{1,0:T(4,128)S(1)} %get-tuple-element.633), kind=kLoop, calls=%fused_computation.26.clone.1 | loop fusion | flops 12582912 | bytes 41951232 | tf_op jit(solution)/shard_map/while/body/eval_jaxpr/while/body/eval_jaxpr/convert_element_type | solution.py:118
  477.2 7.2 fusion.139
  484.3 6.8 fusion.141
  491.1 5.0 fusion.140
  497.6 9.1 fusion.137
  507.5 13.9 %multiply_reduce_fusion.10 = (f32[4,512]{1,0:T(4,128)S(1)}, f32[4,512,2048]{2,1,0:T(8,128)}) fusion(f32[4,512,2048]{2,1,0:T(8,128)} %fusion.137, f32[4,512]{1,0:T(4,128)S(1)} %dynamic-slice_bitcast_fusion.2, f32[512,2048]{1,0:T(8,128)S(1)} %abs_convert_fusion.5, f32[4]{0:T(128)S(1)} %multiply_exponential_fusion.5, ...), kind=kOutput, calls=%fused_computation.27.clone.1 | convolution fusion | flops 566228992 | bytes 40124944 | tf_op jit(solution)/shard_map/while/body/eval_jaxpr/while/body/eval_jaxpr/qhd,khd->hqk/dot_general | solution.py:39
  521.4 15.0 %multiply_convert_fusion.9 = bf16[4,512,2048]{2,1,0:T(8,128)(2,1)} fusion(f32[4,512,2048]{2,1,0:T(8,128)} %get-tuple-element.632, f32[4,512,2048]{2,1,0:T(8,128)} %fusion.137, f32[4,512]{1,0:T(4,128)S(1)} %get-tuple-element.633), kind=kLoop, calls=%fused_computation.26.clone.1 | loop fusion | flops 12582912 | bytes 41951232 | tf_op jit(solution)/shard_map/while/body/eval_jaxpr/while/body/eval_jaxpr/convert_element_type | solution.py:118
  536.3 7.2 fusion.139
  543.5 6.8 fusion.141
  550.3 5.0 fusion.140
  563.6 39.8 %all_to_all.50 = bf16[4,1,512,3,1,256]{2,5,3,4,1,0:T(8,128)(2,1)S(1)} all-to-all(bf16[4,1,512,3,1,256]{2,5,3,4,1,0:T(8,128)(2,1)S(1)} %pad_maximum_fusion.1), channel_id=1, replica_groups=mesh['rows'=8,'seq'=4] {'seq'}, dimensions={0} | all-to-all | bytes 6291456 | tf_op jit(solution)/shard_map/all_to_all | solution.py:245
  606.0 6.8 fusion.69
  612.9 8.6 multiply_reduce_fusion.2
  623.3 5.7 fusion.53
  630.7 11.5 fusion.70
  643.5 11.1 fusion.59
  655.3 10.8 fusion.52
  666.1 43.5 %all-reduce.4 = (f32[1024]{0:T(1024)S(1)}, f32[1024]{0:T(1024)S(1)}, f32[4096]{0:T(1024)S(1)}, f32[1024]{0:T(1024)S(1)}) all-reduce(f32[1024]{0:T(1024)S(1)} %get-tuple-element.369, f32[1024]{0:T(1024)S(1)} %copy-done.41, f32[4096]{0:T(1024)S(1)} %copy-done.35, ...), channel_id=3, replica_groups=mesh['rows'=8,'seq'=4] {'rows','seq'}, use_global_device_ids=true, to_apply=%region_17.18.clone | all-reduce | flops 7168 | bytes 57344
  718.1 50.7 %reduce-scatter.8.cloned.1.call-done = f32[32,3072]{1,0:T(8,128)} async-done(((f32[1024,3072]{1,0:T(8,128)}), f32[32,3072]{1,0:T(8,128)}) %reduce-scatter.8.cloned.1.call-update) | async-done | bytes 393232 | tf_op jit(solution)/shard_map/reduce_scatter | solution.py:269
  768.8 138.5 %reduce-scatter.6.cloned.1.call-done = f32[64,1024]{1,0:T(8,128)} async-done(((f32[2048,1024]{1,0:T(8,128)}), f32[64,1024]{1,0:T(8,128)}) %reduce-scatter.6.cloned.1.call-update) | async-done | bytes 262160 | tf_op jit(solution)/shard_map/reduce_scatter | solution.py:267
  907.3 198.7 %reduce-scatter.12.cloned.1.call-done = f32[32,4096]{1,0:T(8,128)} async-done(((f32[1024,4096]{1,0:T(8,128)}), f32[32,4096]{1,0:T(8,128)}) %reduce-scatter.12.cloned.1.call-update) | async-done | bytes 524304 | tf_op jit(solution)/shard_map/reduce_scatter | solution.py:272
  1106.0 186.7 %reduce-scatter.14.cloned.1.call-done = f32[128,1024]{1,0:T(8,128)} async-done(((f32[4096,1024]{1,0:T(8,128)}), f32[128,1024]{1,0:T(8,128)}) %reduce-scatter.14.cloned.1.call-update) | async-done | bytes 524304 | tf_op jit(solution)/shard_map/reduce_scatter | solution.py:274
  (250 shorter events, 96.9 us)
Async XLA Ops:
  7.2 225.5 %copy-start = (bf16[1024,1024]{1,0:T(8,128)(2,1)S(1)}, bf16[1024,1024]{1,0:T(8,128)(2,1)}, u32[]{:S(2)}) copy-start(bf16[1024,1024]{1,0:T(8,128)(2,1)} %param.25) | copy-start | bytes 6291460
  7.2 5.8 copy-start.42
  7.2 7.3 copy-start.45
  30.5 5.9 copy-start.24
  30.5 41.6 %all-to-all-start = ((bf16[1,512,3,4,256]{4,1,2,0,3:T(8,128)(2,1)}), bf16[1,512,3,4,256]{4,1,2,0,3:T(8,128)(2,1)}, u32[]{:S(2)}, u32[]{:S(2)}) async-start(bf16[1,512,3,4,256]{4,1,2,0,3:T(8,128)(2,1)} %copy.73), calls=%async_computation | async-start | bytes 6291456 | tf_op jit(solution)/shard_map/all_to_all | solution.py:183
  84.3 6.7 copy-start.25
  91.5 2.3 copy-start.4
  93.0 7.1 copy-start.6
  93.8 6.3 copy-start.3
  114.1 2.3 copy-start.4
  115.6 7.1 copy-start.6
  116.4 6.3 copy-start.3
  136.7 2.3 copy-start.4
  138.2 7.1 copy-start.6
  139.0 6.3 copy-start.3
  159.3 2.3 copy-start.4
  160.8 7.1 copy-start.6
  161.6 6.3 copy-start.3
  194.2 18.3 %copy-start.43 = (bf16[1024]{0:T(1024)(128)(2,1)S(1)}, bf16[1024]{0:T(1024)(128)(2,1)}, u32[]{:S(2)}) copy-start(bf16[1024]{0:T(1024)(128)(2,1)} %param.26) | copy-start | bytes 6148
  194.2 18.3 %copy-start.38 = (bf16[4096]{0:T(1024)(128)(2,1)S(1)}, bf16[4096]{0:T(1024)(128)(2,1)}, u32[]{:S(2)}) copy-start(bf16[4096]{0:T(1024)(128)(2,1)} %param.28) | copy-start | bytes 24580
  208.2 18.0 %all-to-all-start.1 = ((bf16[4,2,65536]{2,1,0:T(2,128)(2,1)}), bf16[4,2,65536]{2,1,0:T(2,128)(2,1)S(1)}, u32[]{:S(2)}, u32[]{:S(2)}) async-start(bf16[4,2,65536]{2,1,0:T(2,128)(2,1)} %reshape.630), calls=%async_computation.1 | async-start | bytes 2097152 | tf_op jit(solution)/shard_map/all_to_all | solution.py:191
  212.6 74.8 %copy-start.31 = (f32[1024]{0:T(1024)}, f32[1024]{0:T(1024)S(1)}, u32[]{:S(2)}) copy-start(f32[1024]{0:T(1024)S(1)} %convert_element_type.102) | copy-start | bytes 12292
  235.7 51.8 %copy-start.12 = (f32[512,1024]{1,0:T(8,128)}, f32[512,1024]{1,0:T(8,128)S(1)}, u32[]{:S(2)}) copy-start(f32[512,1024]{1,0:T(8,128)S(1)} %get-tuple-element.454) | copy-start | bytes 6291460
  235.7 51.7 %copy-start.26 = (f32[512]{0:T(512)}, f32[512]{0:T(512)S(1)}, u32[]{:S(2)}) copy-start(f32[512]{0:T(512)S(1)} %broadcast_multiply_fusion.4) | copy-start | bytes 6148
  236.1 51.4 %copy-start.36 = (f32[512]{0:T(512)}, f32[512]{0:T(512)S(1)}, u32[]{:S(2)}) copy-start(f32[512]{0:T(512)S(1)} %add_rsqrt_fusion) | copy-start | bytes 6148
  236.1 27.8 %copy-start.18 = (bf16[1,512,1024]{2,1,0:T(8,128)(2,1)S(1)}, bf16[1,512,1024]{2,1,0:T(8,128)(2,1)}, u32[]{:S(2)}) copy-start(bf16[1,512,1024]{2,1,0:T(8,128)(2,1)} %param.31) | copy-start | bytes 3145732
  277.9 9.6 copy-start.48
  292.5 10.2 copy-start.10
  297.6 19.7 %all-to-all-start.2 = ((bf16[1,512,4,256]{3,1,0,2:T(8,128)(2,1)}), bf16[1,512,4,256]{3,1,0,2:T(8,128)(2,1)}, u32[]{:S(2)}, u32[]{:S(2)}) async-start(bf16[1,512,4,256]{3,1,0,2:T(8,128)(2,1)} %copy.79), calls=%async_computation.2 | async-start | bytes 2097152 | tf_op jit(solution)/shard_map/all_to_all | solution.py:222
  302.7 415.4 %reduce-scatter.10.cloned.1.call-start = ((), (), s32[]{:S(2)}) async-start(), calls=%async_computation.11 | async-start | bytes 4325376 | tf_op jit(solution)/shard_map/reduce_scatter | solution.py:270
  305.9 13.6 %copy-start.5 = (bf16[2048,4,64]{0,2,1:T(8,128)(2,1)S(1)}, bf16[2048,4,64]{0,2,1:T(8,128)(2,1)}, u32[]{:S(2)}) copy-start(bf16[2048,4,64]{0,2,1:T(8,128)(2,1)} %get-tuple-element.723) | copy-start | bytes 3145732
  305.9 13.6 %copy-start.8 = (bf16[2048,4,64]{0,2,1:T(8,128)(2,1)S(1)}, bf16[2048,4,64]{0,2,1:T(8,128)(2,1)}, u32[]{:S(2)}) copy-start(bf16[2048,4,64]{0,2,1:T(8,128)(2,1)} %get-tuple-element.724) | copy-start | bytes 3145732
  306.0 462.8 %reduce-scatter.8.cloned.1.call-start = ((), (), s32[]{:S(2)}) async-start(), calls=%async_computation.10 | async-start | bytes 12976128 | tf_op jit(solution)/shard_map/reduce_scatter | solution.py:269
  344.9 21.7 %copy-start.20 = (bf16[4,512,4,64]{1,3,2,0:T(8,128)(2,1)S(1)}, bf16[4,512,4,64]{1,3,2,0:T(8,128)(2,1)}, u32[]{:S(2)}) copy-start(bf16[4,512,4,64]{1,3,2,0:T(8,128)(2,1)} %get-tuple-element.689) | copy-start | bytes 3145732 | tf_op jit(solution)/shard_map/while/body/eval_jaxpr/while
  360.0 13.4 %copy-start.2 = (f32[4,512,2048]{2,1,0:T(8,128)S(1)}, f32[4,512,2048]{2,1,0:T(8,128)}, u32[]{:S(2)}) copy-start(f32[4,512,2048]{2,1,0:T(8,128)} %get-tuple-element.632) | copy-start | bytes 50331652 | tf_op jit(solution)/shard_map/while/body/eval_jaxpr/while
  373.4 4.1 copy-start.21
  402.9 22.2 %copy-start.20 = (bf16[4,512,4,64]{1,3,2,0:T(8,128)(2,1)S(1)}, bf16[4,512,4,64]{1,3,2,0:T(8,128)(2,1)}, u32[]{:S(2)}) copy-start(bf16[4,512,4,64]{1,3,2,0:T(8,128)(2,1)} %get-tuple-element.689) | copy-start | bytes 3145732 | tf_op jit(solution)/shard_map/while/body/eval_jaxpr/while
  417.9 14.0 %copy-start.2 = (f32[4,512,2048]{2,1,0:T(8,128)S(1)}, f32[4,512,2048]{2,1,0:T(8,128)}, u32[]{:S(2)}) copy-start(f32[4,512,2048]{2,1,0:T(8,128)} %get-tuple-element.632) | copy-start | bytes 50331652 | tf_op jit(solution)/shard_map/while/body/eval_jaxpr/while
  431.9 5.0 copy-start.21
  462.2 22.1 %copy-start.20 = (bf16[4,512,4,64]{1,3,2,0:T(8,128)(2,1)S(1)}, bf16[4,512,4,64]{1,3,2,0:T(8,128)(2,1)}, u32[]{:S(2)}) copy-start(bf16[4,512,4,64]{1,3,2,0:T(8,128)(2,1)} %get-tuple-element.689) | copy-start | bytes 3145732 | tf_op jit(solution)/shard_map/while/body/eval_jaxpr/while
  477.2 14.0 %copy-start.2 = (f32[4,512,2048]{2,1,0:T(8,128)S(1)}, f32[4,512,2048]{2,1,0:T(8,128)}, u32[]{:S(2)}) copy-start(f32[4,512,2048]{2,1,0:T(8,128)} %get-tuple-element.632) | copy-start | bytes 50331652 | tf_op jit(solution)/shard_map/while/body/eval_jaxpr/while
  491.1 5.0 copy-start.21
  521.4 22.1 %copy-start.20 = (bf16[4,512,4,64]{1,3,2,0:T(8,128)(2,1)S(1)}, bf16[4,512,4,64]{1,3,2,0:T(8,128)(2,1)}, u32[]{:S(2)}) copy-start(bf16[4,512,4,64]{1,3,2,0:T(8,128)(2,1)} %get-tuple-element.689) | copy-start | bytes 3145732 | tf_op jit(solution)/shard_map/while/body/eval_jaxpr/while
  536.3 14.0 %copy-start.2 = (f32[4,512,2048]{2,1,0:T(8,128)S(1)}, f32[4,512,2048]{2,1,0:T(8,128)}, u32[]{:S(2)}) copy-start(f32[4,512,2048]{2,1,0:T(8,128)} %get-tuple-element.632) | copy-start | bytes 50331652 | tf_op jit(solution)/shard_map/while/body/eval_jaxpr/while
  550.3 5.0 copy-start.21
  555.5 5.0 copy-start.7
  603.4 2.6 copy-start.15
  603.4 2.6 copy-start.29
  603.4 2.6 copy-start.34
  603.4 2.6 copy-start.40
  612.8 8.7 copy-start.11
  612.8 294.4 %reduce-scatter.6.cloned.1.call-start = ((), (), s32[]{:S(2)}) async-start(), calls=%async_computation.9 | async-start | bytes 8650752 | tf_op jit(solution)/shard_map/reduce_scatter | solution.py:267
  612.9 8.7 copy-start.16
  621.5 1.8 copy-start.46
  621.5 1.8 copy-start.47
  629.0 1.7 copy-start.32
  629.0 1.7 copy-start.37
  629.0 476.9 %reduce-scatter.12.cloned.1.call-start = ((), (), s32[]{:S(2)}) async-start(), calls=%async_computation.12 | async-start | bytes 17301504 | tf_op jit(solution)/shard_map/reduce_scatter | solution.py:272
  642.2 650.5 %reduce-scatter.14.cloned.1.call-start = ((), (), s32[]{:S(2)}) async-start(), calls=%async_computation.13 | async-start | bytes 17301504 | tf_op jit(solution)/shard_map/reduce_scatter | solution.py:274
  655.3 10.8 copy-start.30
  655.3 10.8 copy-start.35
  655.3 10.8 copy-start.41
  655.3 56.6 %copy-start.23 = (bf16[512,1024]{1,0:T(8,128)(2,1)S(1)}, bf16[512,1024]{1,0:T(8,128)(2,1)}, u32[]{:S(2)}) copy-start(bf16[512,1024]{1,0:T(8,128)(2,1)} %copy-done.22) | copy-start | bytes 3145732
  711.9 580.8 %copy-start.1 = (bf16[1024,1024]{1,0:T(8,128)(2,1)S(1)}, bf16[1024,1024]{1,0:T(8,128)(2,1)}, u32[]{:S(2)}) copy-start(bf16[1024,1024]{1,0:T(8,128)(2,1)} %param.25) | copy-start | bytes 6291460
  (11 other events, 13.4 us)
Sparse Core Ops, SparseCore 0:
  306.4 126.9 reduce-scatter.9
  612.9 155.8 reduce-scatter.7
  771.8 135.4 reduce-scatter.5
  910.1 195.8 reduce-scatter.11
  1108.8 183.8 reduce-scatter.13
